TPU v7x, 32 devices: a whole 2x2x4 slice. The times are simulated.
32 devices in a mesh: seq: 8 (over y, x, core), head: 4 (over z).
Axes of the slice: x: 2, y: 2, z: 4, core: 2. Of those that a mesh axis runs over, the one named last changes fastest.
Arguments:
- query_rows: bfloat16 [2048, 3072], P('seq', 'head'), may hold values from -60 to 60
- key_rows: bfloat16 [2048, 3072], P('seq', 'head'), may hold values from -5 to 5
- value_rows: bfloat16 [2048, 3072], P('seq', 'head'), may hold values from -6 to 6
- grad_out: bfloat16 [2048, 3072], P('seq', 'head'), may hold values from -6 to 6
Outputs:
- attended: bfloat16 [2048, 3072], P('seq', 'head')
- grad_query: bfloat16 [2048, 3072], P('seq', 'head')
- grad_keys: bfloat16 [2048, 3072], P('seq', 'head')
- grad_values: bfloat16 [2048, 3072], P('seq', 'head')
All inputs are finite; a program needn't handle non-finite values.
Results may differ from a plain program's by a relative error of at most 0.0081.
Values may be sent and summed in bfloat16 or wider, within the bound.
A program may use at most 64 MiB of HBM per device.

v0:
```python
import jax
import jax.numpy as jnp
from jax import lax
from jax.sharding import PartitionSpec as P

HEAD_DIM = 128
BLOCK = 128
STRIDE = 512


NEG_FILL = -1e30


def swapped(value, axis, stride):
    mask = 2**stride
    pairs = [(source, source ^ mask) for source in range(lax.axis_size(axis))]
    return lax.ppermute(value, axis, pairs)


def passed_along(shard, axis, by):
    size = lax.axis_size(axis)
    pairs = [(i, i + by) for i in range(size) if 0 <= i + by < size]
    return lax.ppermute(shard, axis, pairs)


def attend(queries, keyset, valueset, upstream, allowed, score_scale):
    scores = (
        jnp.einsum("...qd,...kd->...qk", queries, keyset, preferred_element_type=jnp.float32)
        * score_scale
    )
    scores = jnp.where(allowed, scores, NEG_FILL)
    row_peak = jnp.max(scores, axis=-1, keepdims=True)
    log_total = row_peak + jnp.log(jnp.sum(jnp.exp(scores - row_peak), axis=-1, keepdims=True))
    weights = jnp.exp(scores - log_total)
    rounded_weights = weights.astype(jnp.bfloat16)
    attended = jnp.einsum(
        "...qk,...kd->...qd", rounded_weights, valueset, preferred_element_type=jnp.float32
    ).astype(jnp.bfloat16)
    if upstream is None:
        return attended
    out_float = lax.optimization_barrier(attended).astype(jnp.float32)
    row_dots = jnp.sum(upstream.astype(jnp.float32) * out_float, axis=-1, keepdims=True)
    weight_grads = jnp.einsum(
        "...qd,...kd->...qk", upstream, valueset, preferred_element_type=jnp.float32
    )
    score_grads = (weights * (weight_grads - row_dots)).astype(jnp.bfloat16)
    grad_query = (
        jnp.einsum("...qk,...kd->...qd", score_grads, keyset, preferred_element_type=jnp.float32)
        * score_scale
    ).astype(jnp.bfloat16)
    grad_keys = (
        jnp.einsum("...qk,...qd->...kd", score_grads, queries, preferred_element_type=jnp.float32)
        * score_scale
    )
    grad_values = jnp.einsum(
        "...qk,...qd->...kd", rounded_weights, upstream, preferred_element_type=jnp.float32
    )
    return (attended, grad_query, grad_keys, grad_values)


def shards(query_rows, key_rows, value_rows, grad_out):
    local_rows, full_width = query_rows.shape
    half_heads = full_width // (2 * HEAD_DIM)
    score_scale = HEAD_DIM ** (-0.5)
    head_count = lax.axis_size("head")
    pair_bit = head_count.bit_length() - 2
    band_holder = lax.axis_index("head") < head_count // 2

    def halves(tensor):
        return tensor.reshape(local_rows, 2, half_heads, HEAD_DIM)

    split_in = [halves(tensor) for tensor in (query_rows, key_rows, value_rows, grad_out)]
    outgoing = [jnp.where(band_holder, tensor[:, 1], tensor[:, 0]) for tensor in split_in]
    staying = [jnp.where(band_holder, tensor[:, 0], tensor[:, 1]) for tensor in split_in]
    incoming = swapped((outgoing[0], outgoing[1], outgoing[2], outgoing[3]), "head", pair_bit)
    band_in = [
        jnp.where(band_holder, own_part, other_part)
        for own_part, other_part in zip(staying, incoming)
    ]
    stride_in = [
        jnp.where(band_holder, other_part, own_part)
        for own_part, other_part in zip(staying, incoming)
    ]
    block_count = local_rows // BLOCK
    band_query, band_keys, band_values, band_grads = band_in
    before_rows = passed_along(
        (band_keys[local_rows - BLOCK :], band_values[local_rows - BLOCK :]), "seq", 1
    )

    def blocked(tensor):
        return jnp.swapaxes(tensor.reshape(block_count, BLOCK, half_heads, HEAD_DIM), 1, 2)

    def windowed(earlier, tensor):
        joined = jnp.concatenate([earlier, tensor], 0).reshape(
            block_count + 1, BLOCK, half_heads, HEAD_DIM
        )
        return jnp.swapaxes(jnp.concatenate([joined[:-1], joined[1:]], 1), 1, 2)

    anchor = lax.axis_index("seq") * local_rows
    row_pos = jnp.arange(BLOCK)[:, None]
    key_pos = jnp.arange(2 * BLOCK)[None, :]
    block_pos = jnp.arange(block_count)[:, None, None, None]
    allowed = (
        (key_pos > row_pos)
        & (key_pos <= row_pos + BLOCK)
        & (anchor + (block_pos - 1) * BLOCK + key_pos >= 0)
    )
    band_out, band_dq, key_terms, value_terms = attend(
        blocked(band_query),
        windowed(before_rows[0], band_keys),
        windowed(before_rows[1], band_values),
        blocked(band_grads),
        allowed,
        score_scale,
    )

    def unblocked(tensor):
        return jnp.swapaxes(tensor, 1, 2).reshape(local_rows, half_heads, HEAD_DIM)

    def folded(term_sums):
        spread = jnp.swapaxes(term_sums, 1, 2)
        zero_block = jnp.zeros((1, BLOCK, half_heads, HEAD_DIM), jnp.float32)
        return jnp.concatenate([spread[:, :BLOCK], zero_block], 0) + jnp.concatenate(
            [zero_block, spread[:, BLOCK:]], 0
        )

    key_total = folded(key_terms)
    value_total = folded(value_terms)
    after_terms = (
        passed_along(key_total[0].astype(jnp.bfloat16), "seq", -1).astype(jnp.float32),
        passed_along(value_total[0].astype(jnp.bfloat16), "seq", -1).astype(jnp.float32),
    )
    band_dk = (
        key_total[1:]
        .at[block_count - 1]
        .add(after_terms[0])
        .reshape(local_rows, half_heads, HEAD_DIM)
        .astype(jnp.bfloat16)
    )
    band_dv = (
        value_total[1:]
        .at[block_count - 1]
        .add(after_terms[1])
        .reshape(local_rows, half_heads, HEAD_DIM)
        .astype(jnp.bfloat16)
    )
    band_results = (unblocked(band_out), unblocked(band_dq), band_dk, band_dv)
    seq_count = lax.axis_size("seq")
    group_count = STRIDE // seq_count
    group_span = local_rows // group_count

    def offset_in(tensor):
        return tensor.reshape(local_rows // seq_count, seq_count, half_heads, HEAD_DIM)

    def regroup(tensor):
        return jnp.transpose(
            tensor.reshape(group_span, group_count, tensor.shape[2], HEAD_DIM), (1, 2, 0, 3)
        )

    def restore(tensor):
        return jnp.transpose(tensor, (2, 0, 1, 3)).reshape(local_rows, 1, tensor.shape[1], HEAD_DIM)

    causal_mask = jnp.arange(group_span)[None, :] <= jnp.arange(group_span)[:, None]
    stride_query, stride_keys, stride_values, stride_grads = [
        offset_in(tensor) for tensor in stride_in
    ]
    pieces = (
        lax.all_to_all(stride_query, "seq", split_axis=1, concat_axis=0, tiled=True),
        lax.all_to_all(stride_keys, "seq", split_axis=1, concat_axis=0, tiled=True),
        lax.all_to_all(stride_values, "seq", split_axis=1, concat_axis=0, tiled=True),
    )
    attended = attend(
        regroup(pieces[0]), regroup(pieces[1]), regroup(pieces[2]), None, causal_mask, score_scale
    )
    stride_out = lax.all_to_all(restore(attended), "seq", split_axis=0, concat_axis=1, tiled=True)
    pieces = (
        lax.all_to_all(stride_query, "seq", split_axis=1, concat_axis=0, tiled=True),
        lax.all_to_all(stride_keys, "seq", split_axis=1, concat_axis=0, tiled=True),
        lax.all_to_all(stride_values, "seq", split_axis=1, concat_axis=0, tiled=True),
        lax.all_to_all(stride_grads, "seq", split_axis=1, concat_axis=0, tiled=True),
    )
    results = attend(
        regroup(pieces[0]),
        regroup(pieces[1]),
        regroup(pieces[2]),
        regroup(pieces[3]),
        causal_mask,
        score_scale,
    )
    stride_dq = lax.all_to_all(restore(results[1]), "seq", split_axis=0, concat_axis=1, tiled=True)
    stride_dk = lax.all_to_all(
        restore(results[2].astype(jnp.bfloat16)), "seq", split_axis=0, concat_axis=1, tiled=True
    )
    stride_dv = lax.all_to_all(
        restore(results[3].astype(jnp.bfloat16)), "seq", split_axis=0, concat_axis=1, tiled=True
    )
    stride_results = tuple(
        (
            tensor.reshape(local_rows, half_heads, HEAD_DIM)
            for tensor in (stride_out, stride_dq, stride_dk, stride_dv)
        )
    )
    send_back = [
        jnp.where(band_holder, stride_part, band_part)
        for band_part, stride_part in zip(band_results, stride_results)
    ]
    keep_back = [
        jnp.where(band_holder, band_part, stride_part)
        for band_part, stride_part in zip(band_results, stride_results)
    ]
    returned = swapped((send_back[0], send_back[1], send_back[2], send_back[3]), "head", pair_bit)
    outputs = []
    for kept_part, got_part in zip(keep_back, returned):
        first_half = jnp.where(band_holder, kept_part, got_part)
        second_half = jnp.where(band_holder, got_part, kept_part)
        outputs.append(jnp.stack([first_half, second_half], 1).reshape(local_rows, full_width))
    return (outputs[0], outputs[1], outputs[2], outputs[3])


def solution(mesh):
    return jax.shard_map(
        shards,
        mesh=mesh,
        in_specs=(P("seq", "head"), P("seq", "head"), P("seq", "head"), P("seq", "head")),
        out_specs=(P("seq", "head"), P("seq", "head"), P("seq", "head"), P("seq", "head")),
        check_vma=False,
    )
```

profile of v0, /device:TPU:0, one launch (start us, length us, event | category | flops | bytes accessed | tf_op | source)
XLA Modules:
  0.0 170.6 jit_solution(14314037883619302063)
XLA Ops:
  0.6 1.2 copy.304
  1.9 4.1 %collective-permute-start = (bf16[256,3,128]{0,2,1:T(8,128)(2,1)S(1)}, bf16[256,3,128]{0,2,1:T(8,128)(2,1)S(1)}, u32[]{:S(2)}, u32[]{:S(2)}) collective-permute-start(bf16[256,3,128]{0,2,1:T(8,128)(2,1)S(1)} %select_bitcast_fusion.11), channel_id=1, source_target_pairs={{0,2},{1,3},{2,0},{3,1},{4,6},{5,7},{6,4},{7,5},{8,10},{9,11},{10,... | collective-permute-start | bytes 589832 | tf_op jit(solution)/shard_map/ppermute | solution.py:17
  7.3 2.1 %collective-permute-start.3 = (bf16[256,3,128]{0,2,1:T(8,128)(2,1)S(1)}, bf16[256,3,128]{0,2,1:T(8,128)(2,1)S(1)}, u32[]{:S(2)}, u32[]{:S(2)}) collective-permute-start(bf16[256,3,128]{0,2,1:T(8,128)(2,1)S(1)} %select_bitcast_fusion.9), channel_id=1, source_target_pairs={{0,2},{1,3},{2,0},{3,1},{4,6},{5,7},{6,4},{7,5},{8,10},{9,11},{10,... | collective-permute-start | bytes 589832 | tf_op jit(solution)/shard_map/ppermute | solution.py:17
  9.7 1.0 collective-permute-start.6
  11.5 21.3 %collective-permute-done.1 = bf16[256,3,128]{0,2,1:T(8,128)(2,1)S(1)} collective-permute-done((bf16[256,3,128]{0,2,1:T(8,128)(2,1)S(1)}, bf16[256,3,128]{0,2,1:T(8,128)(2,1)S(1)}, u32[]{:S(2)}, u32[]{:S(2)}) %collective-permute-start.1) | collective-permute-done | bytes 196640 | tf_op jit(solution)/shard_map/ppermute | solution.py:17
  33.0 4.0 %collective-permute-done.3 = bf16[256,3,128]{0,2,1:T(8,128)(2,1)S(1)} collective-permute-done((bf16[256,3,128]{0,2,1:T(8,128)(2,1)S(1)}, bf16[256,3,128]{0,2,1:T(8,128)(2,1)S(1)}, u32[]{:S(2)}, u32[]{:S(2)}) %collective-permute-start.3) | collective-permute-done | bytes 196640 | tf_op jit(solution)/shard_map/ppermute | solution.py:17
  38.3 4.1 %all-to-all-start = ((bf16[32,8,3,128]{3,0,2,1:T(8,128)(2,1)}), bf16[32,8,3,128]{3,0,2,1:T(8,128)(2,1)S(1)}, u32[]{:S(2)}, u32[]{:S(2)}) async-start(bf16[32,8,3,128]{3,0,2,1:T(8,128)(2,1)} %copy.319), calls=%async_computation | async-start | bytes 393216 | tf_op jit(solution)/shard_map/all_to_all | solution.py:168
  43.2 2.4 %collective-permute-start.2 = (bf16[128,3,128]{0,2,1:T(8,128)(2,1)S(1)}, bf16[128,3,128]{0,2,1:T(8,128)(2,1)S(1)}, u32[]{:S(2)}, u32[]{:S(2)}) collective-permute-start(bf16[128,3,128]{0,2,1:T(8,128)(2,1)S(1)} %slice.170), channel_id=1, source_target_pairs={{0,4},{4,8},{8,12},{12,16},{16,20},{20,24},{24,28},{1,5},{5,9},{9,... | collective-permute-start | bytes 294920 | tf_op jit(solution)/shard_map/ppermute | solution.py:23
  46.5 3.5 %collective-permute-start.4 = (bf16[128,3,128]{0,2,1:T(8,128)(2,1)S(1)}, bf16[128,3,128]{0,2,1:T(8,128)(2,1)S(1)}, u32[]{:S(2)}, u32[]{:S(2)}) collective-permute-start(bf16[128,3,128]{0,2,1:T(8,128)(2,1)S(1)} %slice.173), channel_id=1, source_target_pairs={{0,4},{4,8},{8,12},{12,16},{16,20},{20,24},{24,28},{1,5},{5,9},{9,... | collective-permute-start | bytes 294920 | tf_op jit(solution)/shard_map/ppermute | solution.py:23
  55.8 1.3 collective-permute-start.10
  57.8 6.3 %all-to-all-start.1 = ((bf16[32,8,3,128]{3,0,2,1:T(8,128)(2,1)}), bf16[32,8,3,128]{3,0,2,1:T(8,128)(2,1)S(1)}, u32[]{:S(2)}, u32[]{:S(2)}) async-start(bf16[32,8,3,128]{3,0,2,1:T(8,128)(2,1)} %copy.323), calls=%async_computation.1 | async-start | bytes 393216 | tf_op jit(solution)/shard_map/all_to_all | solution.py:169
  64.8 1.3 collective-permute-start.8
  66.3 4.0 %all-to-all-done.1 = bf16[32,8,3,128]{3,0,2,1:T(8,128)(2,1)S(1)} async-done(((bf16[32,8,3,128]{3,0,2,1:T(8,128)(2,1)}), bf16[32,8,3,128]{3,0,2,1:T(8,128)(2,1)S(1)}, u32[]{:S(2)}, u32[]{:S(2)}) %all-to-all-start.1) | async-done | bytes 196640 | tf_op jit(solution)/shard_map/all_to_all | solution.py:169
  70.4 3.4 %all-to-all-start.2 = ((bf16[32,8,3,128]{3,0,2,1:T(8,128)(2,1)}), bf16[32,8,3,128]{3,0,2,1:T(8,128)(2,1)S(1)}, u32[]{:S(2)}, u32[]{:S(2)}) async-start(bf16[32,8,3,128]{3,0,2,1:T(8,128)(2,1)} %copy.328), calls=%async_computation.2 | async-start | bytes 393216 | tf_op jit(solution)/shard_map/all_to_all | solution.py:170
  75.2 4.7 %all-to-all-done.2 = bf16[32,8,3,128]{3,0,2,1:T(8,128)(2,1)S(1)} async-done(((bf16[32,8,3,128]{3,0,2,1:T(8,128)(2,1)}), bf16[32,8,3,128]{3,0,2,1:T(8,128)(2,1)S(1)}, u32[]{:S(2)}, u32[]{:S(2)}) %all-to-all-start.2) | async-done | bytes 196640 | tf_op jit(solution)/shard_map/all_to_all | solution.py:170
  79.9 3.4 %all-to-all-start.4 = ((bf16[32,8,3,128]{3,0,2,1:T(8,128)(2,1)}), bf16[32,8,3,128]{3,0,2,1:T(8,128)(2,1)S(1)}, u32[]{:S(2)}, u32[]{:S(2)}) async-start(bf16[32,8,3,128]{3,0,2,1:T(8,128)(2,1)} %copy.345), calls=%async_computation.4 | async-start | bytes 393216 | tf_op jit(solution)/shard_map/all_to_all | solution.py:180
  84.0 5.5 %all-to-all-done.4 = bf16[32,8,3,128]{3,0,2,1:T(8,128)(2,1)S(1)} async-done(((bf16[32,8,3,128]{3,0,2,1:T(8,128)(2,1)}), bf16[32,8,3,128]{3,0,2,1:T(8,128)(2,1)S(1)}, u32[]{:S(2)}, u32[]{:S(2)}) %all-to-all-start.4) | async-done | bytes 196640 | tf_op jit(solution)/shard_map/all_to_all | solution.py:180
  89.5 1.0 fusion.7
  91.9 3.4 %all-to-all-start.3 = ((bf16[256,1,3,128]{3,2,1,0:T(4,128)(2,1)}), bf16[256,1,3,128]{3,2,1,0:T(4,128)(2,1)S(1)}, u32[]{:S(2)}, u32[]{:S(2)}) async-start(bf16[256,1,3,128]{3,2,1,0:T(4,128)(2,1)} %copy.333), calls=%async_computation.3 | async-start | bytes 524288 | tf_op jit(solution)/shard_map/all_to_all | solution.py:175
  98.9 3.2 %all-to-all-done.3 = bf16[256,1,3,128]{3,2,1,0:T(4,128)(2,1)S(1)} async-done(((bf16[256,1,3,128]{3,2,1,0:T(4,128)(2,1)}), bf16[256,1,3,128]{3,2,1,0:T(4,128)(2,1)S(1)}, u32[]{:S(2)}, u32[]{:S(2)}) %all-to-all-start.3) | async-done | bytes 196640 | tf_op jit(solution)/shard_map/all_to_all | solution.py:175
  102.1 3.4 %all-to-all-start.7 = ((bf16[256,1,3,128]{3,2,1,0:T(4,128)(2,1)}), bf16[256,1,3,128]{3,2,1,0:T(4,128)(2,1)S(1)}, u32[]{:S(2)}, u32[]{:S(2)}) async-start(bf16[256,1,3,128]{3,2,1,0:T(4,128)(2,1)} %copy.375), calls=%async_computation.7 | async-start | bytes 524288 | tf_op jit(solution)/shard_map/all_to_all | solution.py:194
  107.8 4.7 %all-to-all-done.7 = bf16[256,1,3,128]{3,2,1,0:T(4,128)(2,1)S(1)} async-done(((bf16[256,1,3,128]{3,2,1,0:T(4,128)(2,1)}), bf16[256,1,3,128]{3,2,1,0:T(4,128)(2,1)S(1)}, u32[]{:S(2)}, u32[]{:S(2)}) %all-to-all-start.7) | async-done | bytes 196640 | tf_op jit(solution)/shard_map/all_to_all | solution.py:194
  112.4 3.4 %all-to-all-start.5 = ((bf16[256,1,3,128]{3,2,1,0:T(4,128)(2,1)}), bf16[256,1,3,128]{3,2,1,0:T(4,128)(2,1)S(1)}, u32[]{:S(2)}, u32[]{:S(2)}) async-start(bf16[256,1,3,128]{3,2,1,0:T(4,128)(2,1)} %copy.352), calls=%async_computation.5 | async-start | bytes 524288 | tf_op jit(solution)/shard_map/all_to_all | solution.py:190
  117.0 5.7 %all-to-all-done.5 = bf16[256,1,3,128]{3,2,1,0:T(4,128)(2,1)S(1)} async-done(((bf16[256,1,3,128]{3,2,1,0:T(4,128)(2,1)}), bf16[256,1,3,128]{3,2,1,0:T(4,128)(2,1)S(1)}, u32[]{:S(2)}, u32[]{:S(2)}) %all-to-all-start.5) | async-done | bytes 196640 | tf_op jit(solution)/shard_map/all_to_all | solution.py:190
  122.7 3.6 %all-to-all-start.6 = ((bf16[256,1,3,128]{3,2,1,0:T(4,128)(2,1)}), bf16[256,1,3,128]{3,2,1,0:T(4,128)(2,1)S(1)}, u32[]{:S(2)}, u32[]{:S(2)}) async-start(bf16[256,1,3,128]{3,2,1,0:T(4,128)(2,1)} %copy.364), calls=%async_computation.6 | async-start | bytes 524288 | tf_op jit(solution)/shard_map/all_to_all | solution.py:191
  128.3 4.7 %all-to-all-done.6 = bf16[256,1,3,128]{3,2,1,0:T(4,128)(2,1)S(1)} async-done(((bf16[256,1,3,128]{3,2,1,0:T(4,128)(2,1)}), bf16[256,1,3,128]{3,2,1,0:T(4,128)(2,1)S(1)}, u32[]{:S(2)}, u32[]{:S(2)}) %all-to-all-start.6) | async-done | bytes 196640 | tf_op jit(solution)/shard_map/all_to_all | solution.py:191
  133.4 3.0 %collective-permute-start.9 = (bf16[256,3,128]{0,2,1:T(8,128)(2,1)S(1)}, bf16[256,3,128]{0,2,1:T(8,128)(2,1)S(1)}, u32[]{:S(2)}, u32[]{:S(2)}) collective-permute-start(bf16[256,3,128]{0,2,1:T(8,128)(2,1)S(1)} %broadcast_select_fusion.6), channel_id=1, source_target_pairs={{0,2},{1,3},{2,0},{3,1},{4,6},{5,7},{6,4},{7,5},{8,10},{9,11},{10,... | collective-permute-start | bytes 589832 | tf_op jit(solution)/shard_map/ppermute | solution.py:17
  136.5 3.0 %collective-permute-start.11 = (bf16[256,3,128]{0,2,1:T(8,128)(2,1)S(1)}, bf16[256,3,128]{0,2,1:T(8,128)(2,1)S(1)}, u32[]{:S(2)}, u32[]{:S(2)}) collective-permute-start(bf16[256,3,128]{0,2,1:T(8,128)(2,1)S(1)} %broadcast_select_fusion.4), channel_id=1, source_target_pairs={{0,2},{1,3},{2,0},{3,1},{4,6},{5,7},{6,4},{7,5},{8,10},{9,11},{10,... | collective-permute-start | bytes 589832 | tf_op jit(solution)/shard_map/ppermute | solution.py:17
  139.5 17.5 %collective-permute-done.5 = bf16[256,3,128]{0,2,1:T(8,128)(2,1)S(1)} collective-permute-done((bf16[256,3,128]{0,2,1:T(8,128)(2,1)S(1)}, bf16[256,3,128]{0,2,1:T(8,128)(2,1)S(1)}, u32[]{:S(2)}, u32[]{:S(2)}) %collective-permute-start.5) | collective-permute-done | bytes 196640 | tf_op jit(solution)/shard_map/ppermute | solution.py:17
  158.0 3.2 %collective-permute-done.9 = bf16[256,3,128]{0,2,1:T(8,128)(2,1)S(1)} collective-permute-done((bf16[256,3,128]{0,2,1:T(8,128)(2,1)S(1)}, bf16[256,3,128]{0,2,1:T(8,128)(2,1)S(1)}, u32[]{:S(2)}, u32[]{:S(2)}) %collective-permute-start.9) | collective-permute-done | bytes 196640 | tf_op jit(solution)/shard_map/ppermute | solution.py:17
  161.3 4.2 %collective-permute-done.7 = bf16[256,3,128]{0,2,1:T(8,128)(2,1)S(1)} collective-permute-done((bf16[256,3,128]{0,2,1:T(8,128)(2,1)S(1)}, bf16[256,3,128]{0,2,1:T(8,128)(2,1)S(1)}, u32[]{:S(2)}, u32[]{:S(2)}) %collective-permute-start.7) | collective-permute-done | bytes 196640 | tf_op jit(solution)/shard_map/ppermute | solution.py:17
  167.4 2.2 %collective-permute-done.11 = bf16[256,3,128]{0,2,1:T(8,128)(2,1)S(1)} collective-permute-done((bf16[256,3,128]{0,2,1:T(8,128)(2,1)S(1)}, bf16[256,3,128]{0,2,1:T(8,128)(2,1)S(1)}, u32[]{:S(2)}, u32[]{:S(2)}) %collective-permute-start.11) | collective-permute-done | bytes 196640 | tf_op jit(solution)/shard_map/ppermute | solution.py:17
  (150 shorter events, 29.5 us)
Async XLA Ops:
  1.8 4.2 %copy-start.1 = (bf16[256,768]{1,0:T(8,128)(2,1)S(1)}, bf16[256,768]{1,0:T(8,128)(2,1)}, u32[]{:S(2)}) copy-start(bf16[256,768]{1,0:T(8,128)(2,1)} %param.9) | copy-start | bytes 1179652
  1.9 35.3 %collective-permute-start = (bf16[256,3,128]{0,2,1:T(8,128)(2,1)S(1)}, bf16[256,3,128]{0,2,1:T(8,128)(2,1)S(1)}, u32[]{:S(2)}, u32[]{:S(2)}) collective-permute-start(bf16[256,3,128]{0,2,1:T(8,128)(2,1)S(1)} %select_bitcast_fusion.11), channel_id=1, source_target_pairs={{0,2},{1,3},{2,0},{3,1},{4,6},{5,7},{6,4},{7,5},{8,10},{9,11},{10,... | collective-permute-start | bytes 589832 | tf_op jit(solution)/shard_map/ppermute | solution.py:17
  6.1 1.0 copy-start.2
  6.2 26.6 %collective-permute-start.1 = (bf16[256,3,128]{0,2,1:T(8,128)(2,1)S(1)}, bf16[256,3,128]{0,2,1:T(8,128)(2,1)S(1)}, u32[]{:S(2)}, u32[]{:S(2)}) collective-permute-start(bf16[256,3,128]{0,2,1:T(8,128)(2,1)S(1)} %select_bitcast_fusion.10), channel_id=1, source_target_pairs={{0,2},{1,3},{2,0},{3,1},{4,6},{5,7},{6,4},{7,5},{8,10},{9,11},{10,... | collective-permute-start | bytes 589832 | tf_op jit(solution)/shard_map/ppermute | solution.py:17
  7.3 2.1 %copy-start.3 = (bf16[256,768]{1,0:T(8,128)(2,1)S(1)}, bf16[256,768]{1,0:T(8,128)(2,1)}, u32[]{:S(2)}) copy-start(bf16[256,768]{1,0:T(8,128)(2,1)} %param.11) | copy-start | bytes 1179652
  7.3 29.6 %collective-permute-start.3 = (bf16[256,3,128]{0,2,1:T(8,128)(2,1)S(1)}, bf16[256,3,128]{0,2,1:T(8,128)(2,1)S(1)}, u32[]{:S(2)}, u32[]{:S(2)}) collective-permute-start(bf16[256,3,128]{0,2,1:T(8,128)(2,1)S(1)} %select_bitcast_fusion.9), channel_id=1, source_target_pairs={{0,2},{1,3},{2,0},{3,1},{4,6},{5,7},{6,4},{7,5},{8,10},{9,11},{10,... | collective-permute-start | bytes 589832 | tf_op jit(solution)/shard_map/ppermute | solution.py:17
  9.7 40.4 %collective-permute-start.6 = (bf16[256,3,128]{0,2,1:T(8,128)(2,1)S(1)}, bf16[256,3,128]{0,2,1:T(8,128)(2,1)S(1)}, u32[]{:S(2)}, u32[]{:S(2)}) collective-permute-start(bf16[256,3,128]{0,2,1:T(8,128)(2,1)S(1)} %select_bitcast_fusion.6), channel_id=1, source_target_pairs={{0,2},{1,3},{2,0},{3,1},{4,6},{5,7},{6,4},{7,5},{8,10},{9,11},{10,... | collective-permute-start | bytes 589832 | tf_op jit(solution)/shard_map/ppermute | solution.py:17
  38.3 19.5 %all-to-all-start = ((bf16[32,8,3,128]{3,0,2,1:T(8,128)(2,1)}), bf16[32,8,3,128]{3,0,2,1:T(8,128)(2,1)S(1)}, u32[]{:S(2)}, u32[]{:S(2)}) async-start(bf16[32,8,3,128]{3,0,2,1:T(8,128)(2,1)} %copy.319), calls=%async_computation | async-start | bytes 393216 | tf_op jit(solution)/shard_map/all_to_all | solution.py:168
  43.2 7.9 %collective-permute-start.2 = (bf16[128,3,128]{0,2,1:T(8,128)(2,1)S(1)}, bf16[128,3,128]{0,2,1:T(8,128)(2,1)S(1)}, u32[]{:S(2)}, u32[]{:S(2)}) collective-permute-start(bf16[128,3,128]{0,2,1:T(8,128)(2,1)S(1)} %slice.170), channel_id=1, source_target_pairs={{0,4},{4,8},{8,12},{12,16},{16,20},{20,24},{24,28},{1,5},{5,9},{9,... | collective-permute-start | bytes 294920 | tf_op jit(solution)/shard_map/ppermute | solution.py:23
  46.5 4.8 %collective-permute-start.4 = (bf16[128,3,128]{0,2,1:T(8,128)(2,1)S(1)}, bf16[128,3,128]{0,2,1:T(8,128)(2,1)S(1)}, u32[]{:S(2)}, u32[]{:S(2)}) collective-permute-start(bf16[128,3,128]{0,2,1:T(8,128)(2,1)S(1)} %slice.173), channel_id=1, source_target_pairs={{0,4},{4,8},{8,12},{12,16},{16,20},{20,24},{24,28},{1,5},{5,9},{9,... | collective-permute-start | bytes 294920 | tf_op jit(solution)/shard_map/ppermute | solution.py:23
  51.4 0.8 copy-start.11
  55.8 60.1 %collective-permute-start.10 = (bf16[128,3,128]{2,0,1:T(8,128)(2,1)}, bf16[128,3,128]{2,0,1:T(8,128)(2,1)}, u32[]{:S(2)}, u32[]{:S(2)}) collective-permute-start(bf16[128,3,128]{2,0,1:T(8,128)(2,1)} %fusion.58), channel_id=1, source_target_pairs={{4,0},{8,4},{12,8},{16,12},{20,16},{24,20},{28,24},{5,1},{9,5},{13... | collective-permute-start | bytes 294920 | tf_op jit(solution)/shard_map/ppermute | solution.py:23
  57.8 12.5 %all-to-all-start.1 = ((bf16[32,8,3,128]{3,0,2,1:T(8,128)(2,1)}), bf16[32,8,3,128]{3,0,2,1:T(8,128)(2,1)S(1)}, u32[]{:S(2)}, u32[]{:S(2)}) async-start(bf16[32,8,3,128]{3,0,2,1:T(8,128)(2,1)} %copy.323), calls=%async_computation.1 | async-start | bytes 393216 | tf_op jit(solution)/shard_map/all_to_all | solution.py:169
  64.8 61.5 %collective-permute-start.8 = (bf16[128,3,128]{2,0,1:T(8,128)(2,1)}, bf16[128,3,128]{2,0,1:T(8,128)(2,1)}, u32[]{:S(2)}, u32[]{:S(2)}) collective-permute-start(bf16[128,3,128]{2,0,1:T(8,128)(2,1)} %fusion.57), channel_id=1, source_target_pairs={{4,0},{8,4},{12,8},{16,12},{20,16},{24,20},{28,24},{5,1},{9,5},{13... | collective-permute-start | bytes 294920 | tf_op jit(solution)/shard_map/ppermute | solution.py:23
  66.3 7.5 %copy-start.4 = (bf16[32,8,3,128]{3,0,1,2:T(8,128)(2,1)}, bf16[32,8,3,128]{3,0,1,2:T(8,128)(2,1)S(1)}, u32[]{:S(2)}) copy-start(bf16[32,8,3,128]{3,0,1,2:T(8,128)(2,1)S(1)} %copy.320) | copy-start | bytes 589828
  70.4 9.6 %all-to-all-start.2 = ((bf16[32,8,3,128]{3,0,2,1:T(8,128)(2,1)}), bf16[32,8,3,128]{3,0,2,1:T(8,128)(2,1)S(1)}, u32[]{:S(2)}, u32[]{:S(2)}) async-start(bf16[32,8,3,128]{3,0,2,1:T(8,128)(2,1)} %copy.328), calls=%async_computation.2 | async-start | bytes 393216 | tf_op jit(solution)/shard_map/all_to_all | solution.py:170
  73.8 0.7 copy-start.6
  79.9 9.6 %all-to-all-start.4 = ((bf16[32,8,3,128]{3,0,2,1:T(8,128)(2,1)}), bf16[32,8,3,128]{3,0,2,1:T(8,128)(2,1)S(1)}, u32[]{:S(2)}, u32[]{:S(2)}) async-start(bf16[32,8,3,128]{3,0,2,1:T(8,128)(2,1)} %copy.345), calls=%async_computation.4 | async-start | bytes 393216 | tf_op jit(solution)/shard_map/all_to_all | solution.py:180
  83.3 0.7 copy-start.9
  89.5 1.1 copy-start.10
  91.9 10.3 %all-to-all-start.3 = ((bf16[256,1,3,128]{3,2,1,0:T(4,128)(2,1)}), bf16[256,1,3,128]{3,2,1,0:T(4,128)(2,1)S(1)}, u32[]{:S(2)}, u32[]{:S(2)}) async-start(bf16[256,1,3,128]{3,2,1,0:T(4,128)(2,1)} %copy.333), calls=%async_computation.3 | async-start | bytes 524288 | tf_op jit(solution)/shard_map/all_to_all | solution.py:175
  95.7 0.9 copy-start.8
  97.6 0.9 copy-start.7
  98.9 6.6 %copy-start.5 = (bf16[32,8,3,128]{3,0,1,2:T(8,128)(2,1)S(1)}, bf16[32,8,3,128]{3,0,1,2:T(8,128)(2,1)}, u32[]{:S(2)}) copy-start(bf16[32,8,3,128]{3,0,1,2:T(8,128)(2,1)} %copy-done.4) | copy-start | bytes 589828
  102.1 10.3 %all-to-all-start.7 = ((bf16[256,1,3,128]{3,2,1,0:T(4,128)(2,1)}), bf16[256,1,3,128]{3,2,1,0:T(4,128)(2,1)S(1)}, u32[]{:S(2)}, u32[]{:S(2)}) async-start(bf16[256,1,3,128]{3,2,1,0:T(4,128)(2,1)} %copy.375), calls=%async_computation.7 | async-start | bytes 524288 | tf_op jit(solution)/shard_map/all_to_all | solution.py:194
  107.8 8.1 %copy-start = (bf16[2,128,3,128]{3,1,2,0:T(8,128)(2,1)S(1)}, bf16[2,128,3,128]{3,1,2,0:T(8,128)(2,1)}, u32[]{:S(2)}) copy-start(bf16[2,128,3,128]{3,1,2,0:T(8,128)(2,1)} %fusion.13) | copy-start | bytes 589828
  112.4 10.3 %all-to-all-start.5 = ((bf16[256,1,3,128]{3,2,1,0:T(4,128)(2,1)}), bf16[256,1,3,128]{3,2,1,0:T(4,128)(2,1)S(1)}, u32[]{:S(2)}, u32[]{:S(2)}) async-start(bf16[256,1,3,128]{3,2,1,0:T(4,128)(2,1)} %copy.352), calls=%async_computation.5 | async-start | bytes 524288 | tf_op jit(solution)/shard_map/all_to_all | solution.py:190
  122.7 10.3 %all-to-all-start.6 = ((bf16[256,1,3,128]{3,2,1,0:T(4,128)(2,1)}), bf16[256,1,3,128]{3,2,1,0:T(4,128)(2,1)S(1)}, u32[]{:S(2)}, u32[]{:S(2)}) async-start(bf16[256,1,3,128]{3,2,1,0:T(4,128)(2,1)} %copy.364), calls=%async_computation.6 | async-start | bytes 524288 | tf_op jit(solution)/shard_map/all_to_all | solution.py:191
  133.3 23.7 %collective-permute-start.5 = (bf16[256,3,128]{0,2,1:T(8,128)(2,1)S(1)}, bf16[256,3,128]{0,2,1:T(8,128)(2,1)S(1)}, u32[]{:S(2)}, u32[]{:S(2)}) collective-permute-start(bf16[256,3,128]{0,2,1:T(8,128)(2,1)S(1)} %broadcast_select_fusion.10), channel_id=1, source_target_pairs={{0,2},{1,3},{2,0},{3,1},{4,6},{5,7},{6,4},{7,5},{8,10},{9,11},{10,... | collective-permute-start | bytes 589832 | tf_op jit(solution)/shard_map/ppermute | solution.py:17
  133.4 27.8 %collective-permute-start.9 = (bf16[256,3,128]{0,2,1:T(8,128)(2,1)S(1)}, bf16[256,3,128]{0,2,1:T(8,128)(2,1)S(1)}, u32[]{:S(2)}, u32[]{:S(2)}) collective-permute-start(bf16[256,3,128]{0,2,1:T(8,128)(2,1)S(1)} %broadcast_select_fusion.6), channel_id=1, source_target_pairs={{0,2},{1,3},{2,0},{3,1},{4,6},{5,7},{6,4},{7,5},{8,10},{9,11},{10,... | collective-permute-start | bytes 589832 | tf_op jit(solution)/shard_map/ppermute | solution.py:17
  136.4 29.0 %collective-permute-start.7 = (bf16[256,3,128]{0,2,1:T(8,128)(2,1)S(1)}, bf16[256,3,128]{0,2,1:T(8,128)(2,1)S(1)}, u32[]{:S(2)}, u32[]{:S(2)}) collective-permute-start(bf16[256,3,128]{0,2,1:T(8,128)(2,1)S(1)} %broadcast_select_fusion.8), channel_id=1, source_target_pairs={{0,2},{1,3},{2,0},{3,1},{4,6},{5,7},{6,4},{7,5},{8,10},{9,11},{10,... | collective-permute-start | bytes 589832 | tf_op jit(solution)/shard_map/ppermute | solution.py:17
  136.5 33.0 %collective-permute-start.11 = (bf16[256,3,128]{0,2,1:T(8,128)(2,1)S(1)}, bf16[256,3,128]{0,2,1:T(8,128)(2,1)S(1)}, u32[]{:S(2)}, u32[]{:S(2)}) collective-permute-start(bf16[256,3,128]{0,2,1:T(8,128)(2,1)S(1)} %broadcast_select_fusion.4), channel_id=1, source_target_pairs={{0,2},{1,3},{2,0},{3,1},{4,6},{5,7},{6,4},{7,5},{8,10},{9,11},{10,... | collective-permute-start | bytes 589832 | tf_op jit(solution)/shard_map/ppermute | solution.py:17
where the time goes:
time: 172 us; the launch traced here: 171 us
  waiting for transfers between devices  84.9 us (49%)
  starting transfers between devices  53.7 us (31%)
  local copies, waits for them, and re-layouts  18.8 us (11%)
  other arithmetic  6.73 us (4%)
  matrix products  5.06 us (3%)
    ppermute x8, waiting for transfers between devices, swapped(): return lax.ppermute(value, axis, pairs)  52.3 us
    ppermute x8, starting transfers between devices, swapped(): return lax.ppermute(value, axis, pairs)  14.2 us
    ppermute x4, starting transfers between devices, passed_along(): return lax.ppermute(shard, axis, pairs)  8.49 us
    unnamed x32, local copies, waits for them, and re-layouts  7.97 us
    all_to_all x1, starting transfers between devices, shards(): lax.all_to_all(stride_keys, 'seq', split_axis=1, concat_axis=0, tiled=True)  6.29 us
    all_to_all x1, waiting for transfers between devices, shards(): lax.all_to_all(restore(results[1]), 'seq', split_axis=0, concat_axis=1, t...  5.74 us
    all_to_all x1, waiting for transfers between devices, shards(): lax.all_to_all(stride_grads, 'seq', split_axis=1, concat_axis=0, tiled=True)  5.46 us
    all_to_all x1, waiting for transfers between devices, shards(): lax.all_to_all(stride_values, 'seq', split_axis=1, concat_axis=0, tiled=T...  4.75 us
  transfers between devices with their start and end apart: 20, of which 13 were waited for; matrix products, arithmetic and copies ran while one was open for 15% of the time, Pallas kernels for 0%

commit v1 on v0

--- a/solution.py
+++ b/solution.py
@@ -1,6 +1,10 @@
+import functools
+
 import jax
 import jax.numpy as jnp
 from jax import lax
+from jax.experimental import pallas as pl
+from jax.experimental.pallas import tpu as pltpu
 from jax.sharding import PartitionSpec as P
 
 HEAD_DIM = 128
@@ -58,7 +62,7 @@
     return (attended, grad_query, grad_keys, grad_values)
 
 
-def shards(query_rows, key_rows, value_rows, grad_out):
+def swapped_shards(query_rows, key_rows, value_rows, grad_out):
     local_rows, full_width = query_rows.shape
     half_heads = full_width // (2 * HEAD_DIM)
     score_scale = HEAD_DIM ** (-0.5)
@@ -217,6 +221,369 @@
     return (outputs[0], outputs[1], outputs[2], outputs[3])
 
 
+MESH = pl.DeviceIdType.MESH
+CHUNK_HEADS = 2
+ROW_TILE = 16
+
+
+def lane_dot(left, right):
+    return jnp.sum(left * right, axis=-1, keepdims=True)
+
+
+def as_bf16(tensor):
+    return tensor.astype(jnp.bfloat16).astype(jnp.float32)
+
+
+def strided_tile(span, score_scale, queries, keyset, valueset, upstream):
+    attended, grad_query = [None] * span, [None] * span
+    grad_keys, grad_values = [None] * span, [None] * span
+
+    def plus(total, term):
+        return term if total is None else total + term
+
+    for p in range(span):
+        scores = [lane_dot(queries[p], keyset[j]) * score_scale for j in range(p + 1)]
+        peak = functools.reduce(jnp.maximum, scores)
+        total = functools.reduce(jnp.add, [jnp.exp(score - peak) for score in scores])
+        log_total = peak + jnp.log(total)
+        weights = [jnp.exp(score - log_total) for score in scores]
+        rounded_weights = [as_bf16(weight) for weight in weights]
+        out = None
+        for j in range(p + 1):
+            out = plus(out, rounded_weights[j] * valueset[j])
+            grad_values[j] = plus(grad_values[j], rounded_weights[j] * upstream[p])
+        attended[p] = out.astype(jnp.bfloat16)
+        row_dots = lane_dot(upstream[p], attended[p].astype(jnp.float32))
+        dq = None
+        for j in range(p + 1):
+            weight_grads = lane_dot(upstream[p], valueset[j])
+            score_grads = as_bf16(weights[j] * (weight_grads - row_dots))
+            dq = plus(dq, score_grads * keyset[j])
+            grad_keys[j] = plus(grad_keys[j], score_grads * queries[p])
+        grad_query[p] = dq * score_scale
+    grad_keys = [tensor * score_scale for tensor in grad_keys]
+    return attended, grad_query, grad_keys, grad_values
+
+
+def strided_role(span, hop, ins, outs, gathered, results, sems):
+    in_send, in_recv, out_send, out_recv, own_sem = sems
+    rows, width = ins[0].shape
+    piece = rows // span
+    slab = lax.axis_index("seq")
+    place = slab // hop
+    offset = lax.rem(slab, hop)
+    chunk_cols = CHUNK_HEADS * HEAD_DIM
+    chunks = width // chunk_cols
+    score_scale = HEAD_DIM ** (-0.5)
+
+    def partner(step):
+        return lax.rem(place + step, span)
+
+    def seq_of(member):
+        return {"seq": member * hop + offset}
+
+    barrier = pltpu.get_barrier_semaphore()
+    for step in range(1, span):
+        pl.semaphore_signal(barrier, 1, device_id=seq_of(partner(step)), device_id_type=MESH)
+    pl.semaphore_wait(barrier, span - 1)
+
+    def piece_rows(member):
+        return pl.ds(pl.multiple_of(member * piece, piece), piece)
+
+    own = []
+    for i in range(4):
+        copy = pltpu.make_async_copy(
+            ins[i].at[piece_rows(place)], gathered.at[i, place], own_sem.at[i]
+        )
+        copy.start()
+        own.append(copy)
+    incoming = []
+    for c in range(chunks):
+        cols = pl.ds(c * chunk_cols, chunk_cols)
+        copies = []
+        for step in range(1, span):
+            member = partner(step)
+            for i in range(4):
+                copy = pltpu.make_async_remote_copy(
+                    src_ref=ins[i].at[piece_rows(member), cols],
+                    dst_ref=gathered.at[i, place, :, cols],
+                    send_sem=in_send.at[c, step - 1, i],
+                    recv_sem=in_recv.at[c, step - 1, i],
+                    device_id=seq_of(member),
+                    device_id_type=MESH,
+                )
+                copy.start()
+                copies.append(copy)
+        incoming.append(copies)
+    for copy in own:
+        copy.wait()
+    outgoing = []
+    tiles = piece // ROW_TILE
+    for c in range(chunks):
+        for copy in incoming[c]:
+            copy.wait_recv()
+
+        def body(index, carry, c=c):
+            row = pl.ds(pl.multiple_of(lax.rem(index, tiles) * ROW_TILE, ROW_TILE), ROW_TILE)
+            col = pl.ds(
+                pl.multiple_of(c * chunk_cols + (index // tiles) * HEAD_DIM, HEAD_DIM), HEAD_DIM
+            )
+            loaded = [
+                [gathered[i, j, row, col].astype(jnp.float32) for j in range(span)]
+                for i in range(4)
+            ]
+            made = strided_tile(span, score_scale, *loaded)
+            for i in range(4):
+                for j in range(span):
+                    results[i, j, row, col] = made[i][j].astype(jnp.bfloat16)
+            return carry
+
+        lax.fori_loop(0, tiles * CHUNK_HEADS, body, 0)
+        cols = pl.ds(c * chunk_cols, chunk_cols)
+        for step in range(1, span):
+            member = partner(step)
+            for i in range(4):
+                copy = pltpu.make_async_remote_copy(
+                    src_ref=results.at[i, member, :, cols],
+                    dst_ref=outs[i].at[piece_rows(place), cols],
+                    send_sem=out_send.at[c, step - 1, i],
+                    recv_sem=out_recv.at[c, step - 1, i],
+                    device_id=seq_of(member),
+                    device_id_type=MESH,
+                )
+                copy.start()
+                outgoing.append(copy)
+    for i in range(4):
+        outs[i][piece_rows(place), :] = results[i, place]
+    for copies in incoming:
+        for copy in copies:
+            copy.wait_send()
+    for copy in outgoing:
+        copy.wait()
+
+
+def dot_nt(left, right):
+    return lax.dot_general(left, right, (((1,), (1,)), ((), ())), preferred_element_type=jnp.float32)
+
+
+def dot_nn(left, right):
+    return lax.dot_general(left, right, (((1,), (0,)), ((), ())), preferred_element_type=jnp.float32)
+
+
+def dot_tn(left, right):
+    return lax.dot_general(left, right, (((0,), (0,)), ((), ())), preferred_element_type=jnp.float32)
+
+
+def band_role(ins, outs, halo, held, terms, after, sems):
+    halo_send, halo_recv, after_send, after_recv = sems
+    query_ref, key_ref, value_ref, grad_ref = ins
+    out_ref, dq_ref, dk_ref, dv_ref = outs
+    rows, width = query_ref.shape
+    heads = width // HEAD_DIM
+    blocks = rows // BLOCK
+    slab = lax.axis_index("seq")
+    slabs = lax.axis_size("seq")
+    has_before = slab > 0
+    has_after = slab < slabs - 1
+    score_scale = HEAD_DIM ** (-0.5)
+    before_id = {"seq": jnp.maximum(slab - 1, 0)}
+    after_id = {"seq": jnp.minimum(slab + 1, slabs - 1)}
+
+    barrier = pltpu.get_barrier_semaphore()
+
+    @pl.when(has_before)
+    def _():
+        pl.semaphore_signal(barrier, 1, device_id=before_id, device_id_type=MESH)
+
+    @pl.when(has_after)
+    def _():
+        pl.semaphore_signal(barrier, 1, device_id=after_id, device_id_type=MESH)
+
+    peers = has_before.astype(jnp.int32) + has_after.astype(jnp.int32)
+    pl.semaphore_wait(barrier, peers)
+
+    last_rows = pl.ds(rows - BLOCK, BLOCK)
+    halo_copies = [
+        pltpu.make_async_remote_copy(
+            src_ref=ref.at[last_rows],
+            dst_ref=halo.at[i],
+            send_sem=halo_send.at[i],
+            recv_sem=halo_recv.at[i],
+            device_id=after_id,
+            device_id_type=MESH,
+        )
+        for i, ref in enumerate((key_ref, value_ref))
+    ]
+    after_copies = [
+        pltpu.make_async_remote_copy(
+            src_ref=terms.at[i],
+            dst_ref=after.at[i],
+            send_sem=after_send.at[i],
+            recv_sem=after_recv.at[i],
+            device_id=before_id,
+            device_id_type=MESH,
+        )
+        for i in range(2)
+    ]
+
+    @pl.when(has_after)
+    def _():
+        for copy in halo_copies:
+            copy.start()
+
+    row_pos = lax.broadcasted_iota(jnp.int32, (BLOCK, 2 * BLOCK), 0)
+    key_pos = lax.broadcasted_iota(jnp.int32, (BLOCK, 2 * BLOCK), 1)
+    in_window = (key_pos > row_pos) & (key_pos <= row_pos + BLOCK)
+    in_first = in_window & (slab * rows - BLOCK + key_pos >= 0)
+
+    def block_step(block, allowed, h):
+        col = pl.ds(pl.multiple_of(h * HEAD_DIM, HEAD_DIM), HEAD_DIM)
+        own = pl.ds(block * BLOCK, BLOCK)
+        prev = pl.ds((block - 1) * BLOCK, BLOCK)
+        if block == 0:
+            before_keys, before_values = halo[0, :, col], halo[1, :, col]
+        else:
+            before_keys, before_values = key_ref[prev, col], value_ref[prev, col]
+        keyset = jnp.concatenate([before_keys, key_ref[own, col]], 0)
+        valueset = jnp.concatenate([before_values, value_ref[own, col]], 0)
+        queries, upstream = query_ref[own, col], grad_ref[own, col]
+        scores = jnp.where(allowed, dot_nt(queries, keyset) * score_scale, NEG_FILL)
+        peak = jnp.max(scores, axis=-1, keepdims=True)
+        log_total = peak + jnp.log(jnp.sum(jnp.exp(scores - peak), axis=-1, keepdims=True))
+        weights = jnp.exp(scores - log_total)
+        rounded_weights = weights.astype(jnp.bfloat16)
+        attended = dot_nn(rounded_weights, valueset).astype(jnp.bfloat16)
+        row_dots = lane_dot(upstream.astype(jnp.float32), attended.astype(jnp.float32))
+        weight_grads = dot_nt(upstream, valueset)
+        score_grads = (weights * (weight_grads - row_dots)).astype(jnp.bfloat16)
+        out_ref[own, col] = attended
+        dq_ref[own, col] = (dot_nn(score_grads, keyset) * score_scale).astype(jnp.bfloat16)
+        key_terms = dot_tn(score_grads, queries) * score_scale
+        value_terms = dot_tn(rounded_weights, upstream)
+        for i, sums in enumerate((key_terms, value_terms)):
+            dst = (dk_ref, dv_ref)[i]
+            if block == blocks - 1:
+                held[i, block, :, col] = sums[BLOCK:]
+            else:
+                total = sums[BLOCK:] + held[i, block, :, col]
+                dst[own, col] = total.astype(jnp.bfloat16)
+            if block > 0:
+                held[i, block - 1, :, col] = sums[:BLOCK]
+            else:
+                terms[i, :, col] = sums[:BLOCK].astype(jnp.bfloat16)
+
+    for block in range(blocks - 1, 0, -1):
+
+        def body(h, carry, block=block):
+            block_step(block, in_window, h)
+            return carry
+
+        lax.fori_loop(0, heads, body, 0)
+
+    @pl.when(has_before)
+    def _():
+        for copy in halo_copies:
+            copy.wait_recv()
+
+    @pl.when(jnp.logical_not(has_before))
+    def _():
+        halo[...] = jnp.zeros_like(halo)
+
+    def first_body(h, carry):
+        block_step(0, in_first, h)
+        return carry
+
+    lax.fori_loop(0, heads, first_body, 0)
+
+    @pl.when(has_before)
+    def _():
+        for copy in after_copies:
+            copy.start()
+
+    @pl.when(has_after)
+    def _():
+        for copy in after_copies:
+            copy.wait_recv()
+
+    @pl.when(jnp.logical_not(has_after))
+    def _():
+        after[...] = jnp.zeros_like(after)
+
+    for i, dst in enumerate((dk_ref, dv_ref)):
+        dst[last_rows, :] = (held[i, blocks - 1] + after[i].astype(jnp.float32)).astype(
+            jnp.bfloat16
+        )
+
+    @pl.when(has_before)
+    def _():
+        for copy in after_copies:
+            copy.wait_send()
+
+    @pl.when(has_after)
+    def _():
+        for copy in halo_copies:
+            copy.wait_send()
+
+
+def fused_kernel(span, hop, *refs):
+    ins, outs = refs[:4], refs[4:8]
+    gathered, results, halo, held, terms, after = refs[8:14]
+    sems = refs[14:]
+    is_band = lax.axis_index("head") < lax.axis_size("head") // 2
+
+    @pl.when(is_band)
+    def _():
+        band_role(ins, outs, halo, held, terms, after, sems[5:])
+
+    @pl.when(jnp.logical_not(is_band))
+    def _():
+        strided_role(span, hop, ins, outs, gathered, results, sems[:5])
+
+
+def fused_shards(span, hop, *tensors):
+    rows, width = tensors[0].shape
+    piece = rows // span
+    chunks = width // (CHUNK_HEADS * HEAD_DIM)
+    copy_sems = pltpu.SemaphoreType.DMA((chunks, span - 1, 4))
+    pair_sems = pltpu.SemaphoreType.DMA((2,))
+    vmem = pl.BlockSpec(memory_space=pltpu.VMEM)
+    return tuple(
+        pl.pallas_call(
+            functools.partial(fused_kernel, span, hop),
+            out_shape=[jax.ShapeDtypeStruct((rows, width), jnp.bfloat16)] * 4,
+            in_specs=[vmem] * 4,
+            out_specs=[vmem] * 4,
+            scratch_shapes=[
+                pltpu.VMEM((4, span, piece, width), jnp.bfloat16),
+                pltpu.VMEM((4, span, piece, width), jnp.bfloat16),
+                pltpu.VMEM((2, BLOCK, width), jnp.bfloat16),
+                pltpu.VMEM((2, rows // BLOCK, BLOCK, width), jnp.float32),
+                pltpu.VMEM((2, BLOCK, width), jnp.bfloat16),
+                pltpu.VMEM((2, BLOCK, width), jnp.bfloat16),
+                copy_sems,
+                copy_sems,
+                copy_sems,
+                copy_sems,
+                pltpu.SemaphoreType.DMA((4,)),
+                pair_sems,
+                pair_sems,
+                pair_sems,
+                pair_sems,
+            ],
+            compiler_params=pltpu.CompilerParams(collective_id=0, has_side_effects=True),
+        )(*tensors)
+    )
+
+
+def shards(query_rows, key_rows, value_rows, grad_out):
+    rows = query_rows.shape[0]
+    hop = STRIDE // rows
+    span = lax.axis_size("seq") // hop
+    if span <= 8 and rows % (span * ROW_TILE) == 0:
+        return fused_shards(span, hop, query_rows, key_rows, value_rows, grad_out)
+    return swapped_shards(query_rows, key_rows, value_rows, grad_out)
+
+
 def solution(mesh):
     return jax.shard_map(
         shards,

time: 172 us -> 47.4 us (0.28)
  the two profiles are of different devices: /device:TPU:0 before, /device:TPU:22 now
where the time goes in v1:
time: 47.4 us; the launch traced here: 46.9 us
  Pallas kernels  41.4 us (87%)
  local copies, waits for them, and re-layouts  4.84 us (10%)
  between operations  0.65 us (1%)
    pallas_call x1, Pallas kernels, fused_shards(): pl.pallas_call(functools.partial(fused_kernel, span, hop), out_shape=[jax...  41.4 us
    unnamed x10, local copies, waits for them, and re-layouts  4.84 us

profile of v1, /device:TPU:22, one launch (start us, length us, event | category | flops | bytes accessed | tf_op | source)
XLA Modules:
  0.0 46.9 jit_solution(21978202442346192)
XLA Ops:
  0.6 41.4 %shard_map.75 = (bf16[256,768]{1,0:T(8,128)(2,1)}, bf16[256,768]{1,0:T(8,128)(2,1)}, bf16[256,768]{1,0:T(8,128)(2,1)}, bf16[256,768]{1,0:T(8,128)(2,1)}) custom-call(bf16[256,768]{1,0:T(8,128)(2,1)} %refs_0_.1, bf16[256,768]{1,0:T(8,128)(2,1)} %refs_1_.1, bf16[256,768]{1,0:T(8,128)(2,1)} %refs_2_.1, bf16[256,768]{1,0:T(8,128)(2,1)} %refs_3_.1), custom_call_target="tpu_custom_call" | custom-call | tf_op jit(solution)/shard_map/pallas_call | solution.py:551
  42.1 0.0 copy-start.2
  42.1 1.8 %copy.12 = bf16[256,768]{1,0:T(8,128)(2,1)} copy(bf16[256,768]{1,0:T(8,128)(2,1)} %get-tuple-element.8) | data formatting | bytes 786432
  43.9 0.0 copy-done.2
  43.9 0.0 copy-start.1
  43.9 0.7 %copy.13 = bf16[256,768]{1,0:T(8,128)(2,1)} copy(bf16[256,768]{1,0:T(8,128)(2,1)S(1)} %copy-done.2) | data formatting | bytes 786432
  44.6 0.4 copy-done.1
  45.0 0.0 copy-start
  45.0 0.7 %copy.14 = bf16[256,768]{1,0:T(8,128)(2,1)} copy(bf16[256,768]{1,0:T(8,128)(2,1)S(1)} %copy-done.1) | data formatting | bytes 786432
  45.8 0.4 copy-done
  46.2 0.7 %copy.15 = bf16[256,768]{1,0:T(8,128)(2,1)} copy(bf16[256,768]{1,0:T(8,128)(2,1)S(1)} %copy-done) | data formatting | bytes 786432
Async XLA Ops:
  42.1 1.8 %copy-start.2 = (bf16[256,768]{1,0:T(8,128)(2,1)S(1)}, bf16[256,768]{1,0:T(8,128)(2,1)}, u32[]{:S(2)}) copy-start(bf16[256,768]{1,0:T(8,128)(2,1)} %get-tuple-element.9) | copy-start | bytes 1179652
  43.9 1.1 %copy-start.1 = (bf16[256,768]{1,0:T(8,128)(2,1)S(1)}, bf16[256,768]{1,0:T(8,128)(2,1)}, u32[]{:S(2)}) copy-start(bf16[256,768]{1,0:T(8,128)(2,1)} %get-tuple-element.10) | copy-start | bytes 1179652
  45.0 1.1 %copy-start = (bf16[256,768]{1,0:T(8,128)(2,1)S(1)}, bf16[256,768]{1,0:T(8,128)(2,1)}, u32[]{:S(2)}) copy-start(bf16[256,768]{1,0:T(8,128)(2,1)} %get-tuple-element.11) | copy-start | bytes 1179652

commit v2 on v1

--- a/solution.py
+++ b/solution.py
@@ -540,6 +540,37 @@
         strided_role(span, hop, ins, outs, gathered, results, sems[:5])
 
 
+def place_kernel(*refs):
+    made, outs, held, in_sem, out_sem = refs[:4], refs[4:8], refs[8], refs[9], refs[10]
+    takes = [pltpu.make_async_copy(made[i], held.at[i], in_sem.at[i]) for i in range(4)]
+    gives = [pltpu.make_async_copy(held.at[i], outs[i], out_sem.at[i]) for i in range(4)]
+    for copy in takes:
+        copy.start()
+    for take, give in zip(takes, gives):
+        take.wait()
+        give.start()
+    for copy in gives:
+        copy.wait()
+
+
+def placed(made):
+    anywhere = pl.BlockSpec(memory_space=pl.ANY)
+    shape, dtype = made[0].shape, made[0].dtype
+    return tuple(
+        pl.pallas_call(
+            place_kernel,
+            out_shape=[jax.ShapeDtypeStruct(shape, dtype)] * 4,
+            in_specs=[anywhere] * 4,
+            out_specs=[anywhere] * 4,
+            scratch_shapes=[
+                pltpu.VMEM((4, *shape), dtype),
+                pltpu.SemaphoreType.DMA((4,)),
+                pltpu.SemaphoreType.DMA((4,)),
+            ],
+        )(*made)
+    )
+
+
 def fused_shards(span, hop, *tensors):
     rows, width = tensors[0].shape
     piece = rows // span
@@ -547,7 +578,7 @@
     copy_sems = pltpu.SemaphoreType.DMA((chunks, span - 1, 4))
     pair_sems = pltpu.SemaphoreType.DMA((2,))
     vmem = pl.BlockSpec(memory_space=pltpu.VMEM)
-    return tuple(
+    return placed(
         pl.pallas_call(
             functools.partial(fused_kernel, span, hop),
             out_shape=[jax.ShapeDtypeStruct((rows, width), jnp.bfloat16)] * 4,

time: 47.4 us -> 44.7 us (0.943)
  local copies, waits for them, and re-layouts: 4.84 us -> 0 us
  Pallas kernels: 41.4 us -> 43.6 us
    unnamed x10 -> x0, local copies, waits for them, and re-layouts: 4.84 us -> none
    pallas_call x0 -> x1, Pallas kernels: none -> 2.2 us  [placed(): pl.pallas_call(place_kernel, out_shape=[jax.ShapeDtypeStruct(shape, dtype...]
where the time goes in v2:
time: 44.7 us; the launch traced here: 44.3 us
  Pallas kernels  43.6 us (98%)
  between operations  0.64 us (1%)
    pallas_call x1, Pallas kernels, fused_shards(): pl.pallas_call(functools.partial(fused_kernel, span, hop), out_shape=[jax...  41.4 us
    pallas_call x1, Pallas kernels, placed(): pl.pallas_call(place_kernel, out_shape=[jax.ShapeDtypeStruct(shape, dtype...  2.2 us

profile of v2, /device:TPU:22, one launch (start us, length us, event | category | flops | bytes accessed | tf_op | source)
XLA Modules:
  0.0 44.3 jit_solution(1931890064221085611)
XLA Ops:
  0.6 41.4 %shard_map.75 = (bf16[256,768]{1,0:T(8,128)(2,1)}, bf16[256,768]{1,0:T(8,128)(2,1)}, bf16[256,768]{1,0:T(8,128)(2,1)}, bf16[256,768]{1,0:T(8,128)(2,1)}) custom-call(bf16[256,768]{1,0:T(8,128)(2,1)} %refs_0_.1, bf16[256,768]{1,0:T(8,128)(2,1)} %refs_1_.1, bf16[256,768]{1,0:T(8,128)(2,1)} %refs_2_.1, bf16[256,768]{1,0:T(8,128)(2,1)} %refs_3_.1), custom_call_target="tpu_custom_call" | custom-call | tf_op jit(solution)/shard_map/pallas_call | solution.py:582
  42.1 2.2 %shard_map.76 = (bf16[256,768]{1,0:T(8,128)(2,1)}, bf16[256,768]{1,0:T(8,128)(2,1)}, bf16[256,768]{1,0:T(8,128)(2,1)}, bf16[256,768]{1,0:T(8,128)(2,1)}) custom-call(bf16[256,768]{1,0:T(8,128)(2,1)} %get-tuple-element.8.refs_0_, bf16[256,768]{1,0:T(8,128)(2,1)} %get-tuple-element.9.refs_1_, bf16[256,768]{1,0:T(8,128)(2,1)} %get-tuple-element.10.refs_2_, ...), custom_call_target="tpu_custom_call" | custom-call | tf_op jit(solution)/shard_map/pallas_call | solution.py:560

commit v3 on v2

--- a/solution.py
+++ b/solution.py
@@ -234,132 +234,270 @@
     return tensor.astype(jnp.bfloat16).astype(jnp.float32)
 
 
-def strided_tile(span, score_scale, queries, keyset, valueset, upstream):
+def piece_sizes(rows, span):
+    even = rows // span
+    shift = even // 4 // ROW_TILE * ROW_TILE if span == 4 else 0
+    return [even + shift if t in (0, span - 1) else even - shift for t in range(span)]
+
+
+def needed(source, span):
+    return ((0, 3) if source > 0 else ()) + ((1, 2) if source < span - 1 else ())
+
+
+def returned_to(target, span):
+    return ((0, 1) if target > 0 else ()) + ((2, 3) if target < span - 1 else ())
+
+
+def softmax_weights(scores):
+    peak = functools.reduce(jnp.maximum, scores)
+    total = functools.reduce(jnp.add, [jnp.exp(score - peak) for score in scores])
+    log_total = peak + jnp.log(total)
+    return [jnp.exp(score - log_total) for score in scores]
+
+
+def strided_tile(span, score_scale, queries, keyset, valueset, upstream, last_score, last_grad):
+    last = span - 1
     attended, grad_query = [None] * span, [None] * span
     grad_keys, grad_values = [None] * span, [None] * span
 
     def plus(total, term):
         return term if total is None else total + term
 
-    for p in range(span):
-        scores = [lane_dot(queries[p], keyset[j]) * score_scale for j in range(p + 1)]
-        peak = functools.reduce(jnp.maximum, scores)
-        total = functools.reduce(jnp.add, [jnp.exp(score - peak) for score in scores])
-        log_total = peak + jnp.log(total)
-        weights = [jnp.exp(score - log_total) for score in scores]
+    for p in range(1, span):
+        count = min(p + 1, last)
+        scores = [lane_dot(queries[p], keyset[j]) * score_scale for j in range(count)]
+        grads = [lane_dot(upstream[p], valueset[j]) for j in range(count)]
+        if p == last:
+            scores.append(last_score)
+            grads.append(last_grad)
+        weights = softmax_weights(scores)
         rounded_weights = [as_bf16(weight) for weight in weights]
-        out = None
-        for j in range(p + 1):
+        out, dq = None, None
+        for j in range(count):
             out = plus(out, rounded_weights[j] * valueset[j])
             grad_values[j] = plus(grad_values[j], rounded_weights[j] * upstream[p])
         attended[p] = out.astype(jnp.bfloat16)
-        row_dots = lane_dot(upstream[p], attended[p].astype(jnp.float32))
-        dq = None
-        for j in range(p + 1):
-            weight_grads = lane_dot(upstream[p], valueset[j])
-            score_grads = as_bf16(weights[j] * (weight_grads - row_dots))
+        if p == last:
+            row_dots = functools.reduce(
+                jnp.add, [weight * grad for weight, grad in zip(rounded_weights, grads)]
+            )
+        else:
+            row_dots = lane_dot(upstream[p], attended[p].astype(jnp.float32))
+        for j in range(count):
+            score_grads = as_bf16(weights[j] * (grads[j] - row_dots))
             dq = plus(dq, score_grads * keyset[j])
             grad_keys[j] = plus(grad_keys[j], score_grads * queries[p])
         grad_query[p] = dq * score_scale
-    grad_keys = [tensor * score_scale for tensor in grad_keys]
-    return attended, grad_query, grad_keys, grad_values
-
-
-def strided_role(span, hop, ins, outs, gathered, results, sems):
-    in_send, in_recv, out_send, out_recv, own_sem = sems
+    last_weight = rounded_weights[last]
+    last_score_grad = as_bf16(weights[last] * (grads[last] - row_dots))
+    grad_keys = [tensor if tensor is None else tensor * score_scale for tensor in grad_keys]
+    return (attended, grad_query, grad_keys, grad_values), last_weight, last_score_grad
+
+
+def strided_role(place, span, hop, ins, outs, buffers, sems):
+    gathered, results, pair_in, pair_use, pair_out, pair_back = buffers
+    in_send, in_recv, out_send, out_recv, own_sem, ps_send, ps_recv, pb_send, pb_recv = sems
     rows, width = ins[0].shape
-    piece = rows // span
-    slab = lax.axis_index("seq")
-    place = slab // hop
-    offset = lax.rem(slab, hop)
+    sizes = piece_sizes(rows, span)
+    starts = [sum(sizes[:t]) for t in range(span)]
+    last = span - 1
+    size = sizes[place]
+    offset = lax.rem(lax.axis_index("seq"), hop)
     chunk_cols = CHUNK_HEADS * HEAD_DIM
     chunks = width // chunk_cols
+    heads = width // HEAD_DIM
     score_scale = HEAD_DIM ** (-0.5)
-
-    def partner(step):
-        return lax.rem(place + step, span)
+    others = [(place + step) % span for step in range(1, span)]
+    mine = pl.ds(starts[place], size)
 
     def seq_of(member):
         return {"seq": member * hop + offset}
 
+    def rows_of(member):
+        return pl.ds(starts[member], sizes[member])
+
+    def remote(src, dst, send, recv, member):
+        return pltpu.make_async_remote_copy(
+            src_ref=src,
+            dst_ref=dst,
+            send_sem=send,
+            recv_sem=recv,
+            device_id=seq_of(member),
+            device_id_type=MESH,
+        )
+
     barrier = pltpu.get_barrier_semaphore()
-    for step in range(1, span):
-        pl.semaphore_signal(barrier, 1, device_id=seq_of(partner(step)), device_id_type=MESH)
+    for member in others:
+        pl.semaphore_signal(barrier, 1, device_id=seq_of(member), device_id_type=MESH)
     pl.semaphore_wait(barrier, span - 1)
-
-    def piece_rows(member):
-        return pl.ds(pl.multiple_of(member * piece, piece), piece)
 
     own = []
     for i in range(4):
-        copy = pltpu.make_async_copy(
-            ins[i].at[piece_rows(place)], gathered.at[i, place], own_sem.at[i]
-        )
-        copy.start()
-        own.append(copy)
-    incoming = []
+        own.append(
+            pltpu.make_async_copy(
+                ins[i].at[mine], gathered.at[i, place, pl.ds(0, size)], own_sem.at[i]
+            )
+        )
+        own[-1].start()
+    sent = []
+
+    def send_chunk(c):
+        cols = pl.ds(c * chunk_cols, chunk_cols)
+        for member in others:
+            for i in needed(place, span):
+                copy = remote(
+                    ins[i].at[rows_of(member), cols],
+                    gathered.at[i, place, pl.ds(0, sizes[member]), cols],
+                    in_send.at[c, member, i],
+                    in_recv.at[c, place, i],
+                    member,
+                )
+                copy.start()
+                sent.append(copy)
+
+    send_chunk(0)
+    lanes = lax.broadcasted_iota(jnp.int32, (ROW_TILE, 128), 1)
+    if place == last:
+
+        def pair_body(index, carry):
+            row = pl.ds(pl.multiple_of(index * ROW_TILE, ROW_TILE), ROW_TILE)
+            kept = jnp.zeros((ROW_TILE, 128), jnp.float32)
+            for h in range(heads):
+                col = pl.ds(h * HEAD_DIM, HEAD_DIM)
+                q, k, v, g = [ref[row, col].astype(jnp.float32) for ref in ins]
+                kept = jnp.where(lanes == 2 * h, lane_dot(q, k) * score_scale, kept)
+                kept = jnp.where(lanes == 2 * h + 1, lane_dot(g, v), kept)
+            pair_in[row, :] = kept
+            return carry
+
+        lax.fori_loop(0, rows // ROW_TILE, pair_body, 0)
+        for member in others:
+            copy = remote(
+                pair_in.at[rows_of(member)],
+                pair_use.at[pl.ds(0, sizes[member])],
+                ps_send.at[member],
+                ps_recv.at[0],
+                member,
+            )
+            copy.start()
+            sent.append(copy)
+        pair_use[pl.ds(0, size), :] = pair_in[mine, :]
+    for c in range(1, chunks):
+        send_chunk(c)
+    for copy in own:
+        copy.wait()
+    if place != last:
+        piece = pair_use.at[pl.ds(0, size)]
+        remote(piece, piece, ps_send.at[last], ps_recv.at[0], last).wait_recv()
+    tiles = size // ROW_TILE
     for c in range(chunks):
         cols = pl.ds(c * chunk_cols, chunk_cols)
-        copies = []
-        for step in range(1, span):
-            member = partner(step)
-            for i in range(4):
-                copy = pltpu.make_async_remote_copy(
-                    src_ref=ins[i].at[piece_rows(member), cols],
-                    dst_ref=gathered.at[i, place, :, cols],
-                    send_sem=in_send.at[c, step - 1, i],
-                    recv_sem=in_recv.at[c, step - 1, i],
-                    device_id=seq_of(member),
-                    device_id_type=MESH,
+        for member in others:
+            for i in needed(member, span):
+                piece = gathered.at[i, member, pl.ds(0, size), cols]
+                remote(
+                    piece, piece, in_send.at[c, member, i], in_recv.at[c, member, i], member
+                ).wait_recv()
+        pair_out[c] = jnp.zeros(pair_out.shape[1:], jnp.float32)
+
+        def body(index, carry, c=c):
+            row = pl.ds(pl.multiple_of(lax.rem(index, tiles) * ROW_TILE, ROW_TILE), ROW_TILE)
+            head = index // tiles
+            col = pl.ds(pl.multiple_of(c * chunk_cols + head * HEAD_DIM, HEAD_DIM), HEAD_DIM)
+            loaded = [
+                [
+                    gathered[i, j, row, col].astype(jnp.float32) if i in needed(j, span) else None
+                    for j in range(span)
+                ]
+                for i in range(4)
+            ]
+            pairs = pair_use[row, :]
+            lane = 2 * (c * CHUNK_HEADS + head)
+
+            def at_lane(k):
+                return jnp.sum(jnp.where(lanes == k, pairs, 0.0), axis=-1, keepdims=True)
+
+            made, weight, grad = strided_tile(
+                span, score_scale, *loaded, at_lane(lane), at_lane(lane + 1)
+            )
+            for j in range(span):
+                for i in returned_to(j, span):
+                    results[i, j, row, col] = made[i][j].astype(jnp.bfloat16)
+            kept = pair_out[c, row, :]
+            kept = jnp.where(lanes == 2 * head, weight, kept)
+            pair_out[c, row, :] = jnp.where(lanes == 2 * head + 1, grad, kept)
+            return carry
+
+        lax.fori_loop(0, tiles * CHUNK_HEADS, body, 0)
+        for member in others:
+            for i in returned_to(member, span):
+                copy = remote(
+                    results.at[i, member, pl.ds(0, size), cols],
+                    outs[i].at[mine, cols],
+                    out_send.at[c, member, i],
+                    out_recv.at[c, place, i],
+                    member,
                 )
                 copy.start()
-                copies.append(copy)
-        incoming.append(copies)
-    for copy in own:
-        copy.wait()
-    outgoing = []
-    tiles = piece // ROW_TILE
+                sent.append(copy)
+        if place != last:
+            copy = remote(
+                pair_out.at[c, pl.ds(0, size)],
+                pair_back.at[c, mine],
+                pb_send.at[c],
+                pb_recv.at[c, place],
+                last,
+            )
+            copy.start()
+            sent.append(copy)
+        else:
+            pair_back[c, mine, :] = pair_out[c, pl.ds(0, size), :]
+    for i in returned_to(place, span):
+        outs[i][mine, :] = results[i, place, pl.ds(0, size), :]
+    big = rows // 4
+    big_lanes = lax.broadcasted_iota(jnp.int32, (big, 128), 1)
     for c in range(chunks):
-        for copy in incoming[c]:
-            copy.wait_recv()
-
-        def body(index, carry, c=c):
-            row = pl.ds(pl.multiple_of(lax.rem(index, tiles) * ROW_TILE, ROW_TILE), ROW_TILE)
-            col = pl.ds(
-                pl.multiple_of(c * chunk_cols + (index // tiles) * HEAD_DIM, HEAD_DIM), HEAD_DIM
-            )
-            loaded = [
-                [gathered[i, j, row, col].astype(jnp.float32) for j in range(span)]
-                for i in range(4)
-            ]
-            made = strided_tile(span, score_scale, *loaded)
+        cols = pl.ds(c * chunk_cols, chunk_cols)
+        for member in others:
+            for i in returned_to(place, span):
+                piece = outs[i].at[rows_of(member), cols]
+                remote(
+                    piece, piece, out_send.at[c, member, i], out_recv.at[c, member, i], member
+                ).wait_recv()
+            if place == last:
+                piece = pair_back.at[c, rows_of(member)]
+                remote(piece, piece, pb_send.at[c], pb_recv.at[c, member], member).wait_recv()
+        if place not in (0, last):
+            continue
+
+        def close(index, carry, c=c):
+            row = pl.ds(pl.multiple_of(lax.rem(index, 4) * big, big), big)
+            head = index // 4
+            col = pl.ds(pl.multiple_of(c * chunk_cols + head * HEAD_DIM, HEAD_DIM), HEAD_DIM)
+            q, k, v, g = [ref[row, col].astype(jnp.float32) for ref in ins]
+            if place == last:
+                kept = pair_back[c, row, :]
+                weight, grad = [
+                    jnp.sum(jnp.where(big_lanes == 2 * head + n, kept, 0.0), -1, keepdims=True)
+                    for n in range(2)
+                ]
+                terms = (weight * v, grad * k * score_scale, grad * q * score_scale, weight * g)
+            else:
+                (weight,) = softmax_weights([lane_dot(q, k) * score_scale])
+                out = as_bf16(weight) * v
+                row_dots = lane_dot(g, as_bf16(out))
+                grad = as_bf16(weight * (lane_dot(g, v) - row_dots))
+                terms = (out, grad * k * score_scale, grad * q * score_scale, as_bf16(weight) * g)
             for i in range(4):
-                for j in range(span):
-                    results[i, j, row, col] = made[i][j].astype(jnp.bfloat16)
+                total = terms[i]
+                if i in returned_to(place, span):
+                    total = total + outs[i][row, col].astype(jnp.float32)
+                outs[i][row, col] = total.astype(jnp.bfloat16)
             return carry
 
-        lax.fori_loop(0, tiles * CHUNK_HEADS, body, 0)
-        cols = pl.ds(c * chunk_cols, chunk_cols)
-        for step in range(1, span):
-            member = partner(step)
-            for i in range(4):
-                copy = pltpu.make_async_remote_copy(
-                    src_ref=results.at[i, member, :, cols],
-                    dst_ref=outs[i].at[piece_rows(place), cols],
-                    send_sem=out_send.at[c, step - 1, i],
-                    recv_sem=out_recv.at[c, step - 1, i],
-                    device_id=seq_of(member),
-                    device_id_type=MESH,
-                )
-                copy.start()
-                outgoing.append(copy)
-    for i in range(4):
-        outs[i][piece_rows(place), :] = results[i, place]
-    for copies in incoming:
-        for copy in copies:
-            copy.wait_send()
-    for copy in outgoing:
-        copy.wait()
+        lax.fori_loop(0, 4 * CHUNK_HEADS, close, 0)
+    for copy in sent:
+        copy.wait_send()
 
 
 def dot_nt(left, right):
@@ -527,17 +665,20 @@
 
 def fused_kernel(span, hop, *refs):
     ins, outs = refs[:4], refs[4:8]
-    gathered, results, halo, held, terms, after = refs[8:14]
-    sems = refs[14:]
+    buffers, (halo, held, terms, after) = refs[8:14], refs[14:18]
+    sems = refs[18:]
     is_band = lax.axis_index("head") < lax.axis_size("head") // 2
+    place = lax.axis_index("seq") // hop
 
     @pl.when(is_band)
     def _():
-        band_role(ins, outs, halo, held, terms, after, sems[5:])
-
-    @pl.when(jnp.logical_not(is_band))
-    def _():
-        strided_role(span, hop, ins, outs, gathered, results, sems[:5])
+        band_role(ins, outs, halo, held, terms, after, sems[9:])
+
+    for t in range(span):
+
+        @pl.when(jnp.logical_not(is_band) & (place == t))
+        def _(t=t):
+            strided_role(t, span, hop, ins, outs, buffers, sems[:9])
 
 
 def place_kernel(*refs):
@@ -573,9 +714,9 @@
 
 def fused_shards(span, hop, *tensors):
     rows, width = tensors[0].shape
-    piece = rows // span
+    piece = max(piece_sizes(rows, span))
     chunks = width // (CHUNK_HEADS * HEAD_DIM)
-    copy_sems = pltpu.SemaphoreType.DMA((chunks, span - 1, 4))
+    copy_sems = pltpu.SemaphoreType.DMA((chunks, span, 4))
     pair_sems = pltpu.SemaphoreType.DMA((2,))
     vmem = pl.BlockSpec(memory_space=pltpu.VMEM)
     return placed(
@@ -587,6 +728,10 @@
             scratch_shapes=[
                 pltpu.VMEM((4, span, piece, width), jnp.bfloat16),
                 pltpu.VMEM((4, span, piece, width), jnp.bfloat16),
+                pltpu.VMEM((rows, 128), jnp.float32),
+                pltpu.VMEM((piece, 128), jnp.float32),
+                pltpu.VMEM((chunks, piece, 128), jnp.float32),
+                pltpu.VMEM((chunks, rows, 128), jnp.float32),
                 pltpu.VMEM((2, BLOCK, width), jnp.bfloat16),
                 pltpu.VMEM((2, rows // BLOCK, BLOCK, width), jnp.float32),
                 pltpu.VMEM((2, BLOCK, width), jnp.bfloat16),
@@ -596,6 +741,10 @@
                 copy_sems,
                 copy_sems,
                 pltpu.SemaphoreType.DMA((4,)),
+                pltpu.SemaphoreType.DMA((span,)),
+                pltpu.SemaphoreType.DMA((1,)),
+                pltpu.SemaphoreType.DMA((chunks,)),
+                pltpu.SemaphoreType.DMA((chunks, span)),
                 pair_sems,
                 pair_sems,
                 pair_sems,
@@ -610,7 +759,7 @@
     rows = query_rows.shape[0]
     hop = STRIDE // rows
     span = lax.axis_size("seq") // hop
-    if span <= 8 and rows % (span * ROW_TILE) == 0:
+    if 2 <= span <= 8 and rows % (span * ROW_TILE) == 0:
         return fused_shards(span, hop, query_rows, key_rows, value_rows, grad_out)
     return swapped_shards(query_rows, key_rows, value_rows, grad_out)
 

time: 44.7 us -> 43 us (0.962)
  Pallas kernels: 43.6 us -> 42.2 us
    pallas_call x1, Pallas kernels: 41.4 us -> 40 us  [fused_shards(): pl.pallas_call(functools.partial(fused_kernel, span, hop), out_shape=[jax...]
where the time goes in v3:
time: 43 us; the launch traced here: 42.8 us
  Pallas kernels  42.2 us (98%)
  between operations  0.64 us (1%)
    pallas_call x1, Pallas kernels, fused_shards(): pl.pallas_call(functools.partial(fused_kernel, span, hop), out_shape=[jax...  40 us
    pallas_call x1, Pallas kernels, placed(): pl.pallas_call(place_kernel, out_shape=[jax.ShapeDtypeStruct(shape, dtype...  2.2 us

profile of v3, /device:TPU:22, one launch (start us, length us, event | category | flops | bytes accessed | tf_op | source)
XLA Modules:
  0.0 42.8 jit_solution(7558535514036627110)
XLA Ops:
  0.6 40.0 %shard_map.75 = (bf16[256,768]{1,0:T(8,128)(2,1)}, bf16[256,768]{1,0:T(8,128)(2,1)}, bf16[256,768]{1,0:T(8,128)(2,1)}, bf16[256,768]{1,0:T(8,128)(2,1)}) custom-call(bf16[256,768]{1,0:T(8,128)(2,1)} %refs_0_.1, bf16[256,768]{1,0:T(8,128)(2,1)} %refs_1_.1, bf16[256,768]{1,0:T(8,128)(2,1)} %refs_2_.1, bf16[256,768]{1,0:T(8,128)(2,1)} %refs_3_.1), custom_call_target="tpu_custom_call" | custom-call | tf_op jit(solution)/shard_map/pallas_call | solution.py:723
  40.6 2.2 %shard_map.76 = (bf16[256,768]{1,0:T(8,128)(2,1)}, bf16[256,768]{1,0:T(8,128)(2,1)}, bf16[256,768]{1,0:T(8,128)(2,1)}, bf16[256,768]{1,0:T(8,128)(2,1)}) custom-call(bf16[256,768]{1,0:T(8,128)(2,1)} %get-tuple-element.8.refs_0_, bf16[256,768]{1,0:T(8,128)(2,1)} %get-tuple-element.9.refs_1_, bf16[256,768]{1,0:T(8,128)(2,1)} %get-tuple-element.10.refs_2_, ...), custom_call_target="tpu_custom_call" | custom-call | tf_op jit(solution)/shard_map/pallas_call | solution.py:701

commit v4 on v3

--- a/solution.py
+++ b/solution.py
@@ -682,33 +682,24 @@
 
 
 def place_kernel(*refs):
-    made, outs, held, in_sem, out_sem = refs[:4], refs[4:8], refs[8], refs[9], refs[10]
-    takes = [pltpu.make_async_copy(made[i], held.at[i], in_sem.at[i]) for i in range(4)]
-    gives = [pltpu.make_async_copy(held.at[i], outs[i], out_sem.at[i]) for i in range(4)]
-    for copy in takes:
+    made, outs, out_sem = refs[:4], refs[4:8], refs[8]
+    gives = [pltpu.make_async_copy(made[i], outs[i], out_sem.at[i]) for i in range(4)]
+    for copy in gives:
         copy.start()
-    for take, give in zip(takes, gives):
-        take.wait()
-        give.start()
     for copy in gives:
         copy.wait()
 
 
 def placed(made):
-    anywhere = pl.BlockSpec(memory_space=pl.ANY)
     shape, dtype = made[0].shape, made[0].dtype
     return tuple(
         pl.pallas_call(
             place_kernel,
             out_shape=[jax.ShapeDtypeStruct(shape, dtype)] * 4,
-            in_specs=[anywhere] * 4,
-            out_specs=[anywhere] * 4,
-            scratch_shapes=[
-                pltpu.VMEM((4, *shape), dtype),
-                pltpu.SemaphoreType.DMA((4,)),
-                pltpu.SemaphoreType.DMA((4,)),
-            ],
-        )(*made)
+            in_specs=[pl.BlockSpec(memory_space=pltpu.VMEM)] * 4,
+            out_specs=[pl.BlockSpec(memory_space=pl.ANY)] * 4,
+            scratch_shapes=[pltpu.SemaphoreType.DMA((4,))],
+        )(*[pltpu.with_memory_space_constraint(part, pltpu.VMEM) for part in made])
     )
 
 
@@ -722,7 +713,7 @@
     return placed(
         pl.pallas_call(
             functools.partial(fused_kernel, span, hop),
-            out_shape=[jax.ShapeDtypeStruct((rows, width), jnp.bfloat16)] * 4,
+            out_shape=[pltpu.VMEM((rows, width), jnp.bfloat16)] * 4,
             in_specs=[vmem] * 4,
             out_specs=[vmem] * 4,
             scratch_shapes=[

time: 43 us -> 40.8 us (0.949)
  Pallas kernels: 42.2 us -> 40 us
    pallas_call x1, Pallas kernels: 40 us -> 38.8 us  [fused_shards(): pl.pallas_call(functools.partial(fused_kernel, span, hop), out_shape=[plt...]
    pallas_call x1, Pallas kernels: 2.2 us -> 1.17 us  [placed(): pl.pallas_call(place_kernel, out_shape=[jax.ShapeDtypeStruct(shape, dtype...]
where the time goes in v4:
time: 40.8 us; the launch traced here: 40.6 us
  Pallas kernels  40 us (98%)
  between operations  0.64 us (2%)
    pallas_call x1, Pallas kernels, fused_shards(): pl.pallas_call(functools.partial(fused_kernel, span, hop), out_shape=[plt...  38.8 us
    pallas_call x1, Pallas kernels, placed(): pl.pallas_call(place_kernel, out_shape=[jax.ShapeDtypeStruct(shape, dtype...  1.17 us

profile of v4, /device:TPU:22, one launch (start us, length us, event | category | flops | bytes accessed | tf_op | source)
XLA Modules:
  0.0 40.6 jit_solution(8962410989179358419)
XLA Ops:
  0.6 38.8 %shard_map.75 = (bf16[256,768]{1,0:T(8,128)(2,1)S(1)}, bf16[256,768]{1,0:T(8,128)(2,1)S(1)}, bf16[256,768]{1,0:T(8,128)(2,1)S(1)}, bf16[256,768]{1,0:T(8,128)(2,1)S(1)}) custom-call(bf16[256,768]{1,0:T(8,128)(2,1)} %refs_0_.1, bf16[256,768]{1,0:T(8,128)(2,1)} %refs_1_.1, bf16[256,768]{1,0:T(8,128)(2,1)} %refs_2_.1, bf16[256,768]{1,0:T(8,128)(2,1)} %refs_3_.1), custom_call_target="tpu_custom_call" | custom-call | tf_op jit(solution)/shard_map/pallas_call | solution.py:714
  39.4 1.2 %shard_map.76 = (bf16[256,768]{1,0:T(8,128)(2,1)}, bf16[256,768]{1,0:T(8,128)(2,1)}, bf16[256,768]{1,0:T(8,128)(2,1)}, bf16[256,768]{1,0:T(8,128)(2,1)}) custom-call(bf16[256,768]{1,0:T(8,128)(2,1)S(1)} %get-tuple-element.8.refs_0_, bf16[256,768]{1,0:T(8,128)(2,1)S(1)} %get-tuple-element.9.refs_1_, bf16[256,768]{1,0:T(8,128)(2,1)S(1)} %get-tuple-element.10.refs_2_, ...), custom_call_target="tpu_custom_call" | custom-call | tf_op jit(solution)/shard_map/pallas_call | solution.py:696
